TPU v7x, 128 devices: a whole 4x4x4 slice. The times are simulated.
128 devices in a mesh: ctx: 16 (over z, x_lo, core), tp: 8 (over x_hi, y).
Axes of the slice: x: 4 (x_hi: 2, x_lo: 2; x = x_hi * 2 + x_lo), y: 4, z: 4, core: 2. Of those that a mesh axis runs over, the one named last changes fastest.
Arguments:
- hidden_in: bfloat16 [16384, 5376], P(('ctx', 'tp')), may hold values from -6 to 6
- in_gain: float32 [5376], replicated, may hold values from 0.1 to 1.9
- query_weight: bfloat16 [5376, 4096], P('ctx', 'tp'), may hold values from -0.078125 to 0.078125
- key_weight: bfloat16 [5376, 2048], P('ctx', 'tp'), may hold values from -0.078125 to 0.078125
- value_weight: bfloat16 [5376, 2048], P('ctx', 'tp'), may hold values from -0.078125 to 0.078125
- out_weight: bfloat16 [4096, 5376], P('tp', 'ctx'), may hold values from -0.09375 to 0.09375
- q_gain: float32 [128], replicated, may hold values from 0.5 to 16
- k_gain: float32 [128], replicated, may hold values from 0.5 to 16
- post_gain: float32 [5376], replicated, may hold values from 0.1 to 1.9
Outputs:
- layer_out: bfloat16 [16384, 5376], P(('ctx', 'tp'))
All inputs are finite; a program needn't handle non-finite values.
Results may differ from a plain program's by a relative error of at most 0.015.
The roundings to bfloat16 on the way count: a program that leaves them out, or rounds other values in their place, can miss the bound.
Values may be sent and summed in bfloat16 or wider, within the bound.
A program may use at most 192 MiB of HBM per device.

v0:
```python
import jax
import jax.numpy as jnp
from jax import lax
from jax.sharding import PartitionSpec as P

WINDOW = 1024
SCALAR = 168


def from_behind(array, axis, by):
    peers = lax.axis_size(axis)
    pairs = [(i, i + by) for i in range(peers) if 0 <= i + by < peers]
    return lax.ppermute(array, axis, pairs)


def rms_scale(values, gain):
    return values * lax.rsqrt(jnp.mean(values * values, axis=-1, keepdims=True) + 1e-06) * gain


def rotate(vectors, positions):
    half_dim = vectors.shape[-1] // 2
    frequency = 10000.0 ** (-(jnp.arange(half_dim, dtype=jnp.float32) * 2.0 / vectors.shape[-1]))
    angles = positions.astype(jnp.float32)[:, None] * frequency[None, :]
    cosine = jnp.cos(angles)[:, None, :]
    sine_part = jnp.sin(angles)[:, None, :]
    first_half = vectors[..., :half_dim]
    second_half = vectors[..., half_dim:]
    return jnp.concatenate(
        [
            first_half * cosine - second_half * sine_part,
            second_half * cosine + first_half * sine_part,
        ],
        axis=-1,
    )


def attend(queries, keys, values, query_pos, key_pos):
    row_count, query_heads, head_dim = queries.shape
    key_heads = keys.shape[1]
    group_size = query_heads // key_heads
    grouped = queries.reshape(row_count, key_heads, group_size, head_dim)
    scores = jnp.einsum("rhgd,khd->hgrk", grouped, keys, preferred_element_type=jnp.float32)
    offset = query_pos[:, None] - key_pos[None, :]
    allowed = (offset >= 0) & (offset < WINDOW) & (key_pos[None, :] >= 0)
    scores = jnp.where(allowed, scores * float(SCALAR) ** (-0.5), -1e30)
    row_max = jnp.max(scores, axis=-1, keepdims=True)
    expo = jnp.where(allowed, jnp.exp(scores - row_max), 0.0)
    weights = (expo / jnp.sum(expo, axis=-1, keepdims=True)).astype(jnp.bfloat16)
    mixed = jnp.einsum("hgrk,khd->rhgd", weights, values, preferred_element_type=jnp.float32)
    return mixed.astype(jnp.bfloat16).reshape(row_count, query_heads * head_dim)


def attend_blocks(queries, keys, values, query_pos, key_pos):
    row_count = queries.shape[0]
    piece_rows = min(row_count, 512)
    outputs = []
    for first in range(0, row_count, piece_rows):
        outputs.append(
            attend(
                queries[first : first + piece_rows],
                keys[first : first + piece_rows + WINDOW],
                values[first : first + piece_rows + WINDOW],
                query_pos[first : first + piece_rows],
                key_pos[first : first + piece_rows + WINDOW],
            )
        )
    return jnp.concatenate(outputs, axis=0)


def add_product(left, weight_piece):
    return jnp.dot(left, weight_piece, preferred_element_type=jnp.float32)


def reach_keys(keys, values):
    got_keys, got_values = from_behind((keys, values), "ctx", 1)
    far_keys = [got_keys]
    far_values = [got_values]
    return (
        jnp.concatenate(far_keys + [keys], axis=0),
        jnp.concatenate(far_values + [values], axis=0),
    )


def per_device(
    hidden_in,
    in_gain,
    query_weight,
    key_weight,
    value_weight,
    out_weight,
    q_gain,
    k_gain,
    post_gain,
):
    normed = rms_scale(hidden_in.astype(jnp.float32), in_gain).astype(jnp.bfloat16)
    block = lax.all_gather(normed, "tp", axis=0, tiled=True)
    block_rows = block.shape[0]
    head_dim = q_gain.shape[0]
    block_start = lax.axis_index("ctx") * block_rows
    own_pos = block_start + jnp.arange(block_rows, dtype=jnp.int32)
    wide_pos = block_start - WINDOW + jnp.arange(WINDOW + block_rows, dtype=jnp.int32)
    kv_rows = block.shape[0]
    query_raw = add_product(block, lax.all_gather(query_weight, "ctx", axis=0, tiled=True))
    key_raw = add_product(block, lax.all_gather(key_weight, "ctx", axis=0, tiled=True))
    value_raw = add_product(block, lax.all_gather(value_weight, "ctx", axis=0, tiled=True))
    queries = rotate(
        rms_scale(query_raw.reshape(block_rows, -1, head_dim), q_gain), own_pos
    ).astype(jnp.bfloat16)
    keys = rotate(rms_scale(key_raw.reshape(kv_rows, -1, head_dim), k_gain), own_pos).astype(
        jnp.bfloat16
    )
    values = value_raw.astype(jnp.bfloat16).reshape(kv_rows, -1, head_dim)
    keys, values = reach_keys(keys, values)
    attended = attend_blocks(queries, keys, values, own_pos, wide_pos)
    out_full = lax.all_gather(out_weight, "ctx", axis=1, tiled=True)
    projected = lax.psum_scatter(
        jnp.dot(attended, out_full, preferred_element_type=jnp.float32).astype(jnp.bfloat16),
        "tp",
        scatter_dimension=0,
        tiled=True,
    ).astype(jnp.float32)
    return (hidden_in.astype(jnp.float32) + rms_scale(projected, post_gain)).astype(jnp.bfloat16)


def solution(mesh):
    in_specs = (
        P(("ctx", "tp"), None),
        P(),
        P("ctx", "tp"),
        P("ctx", "tp"),
        P("ctx", "tp"),
        P("tp", "ctx"),
        P(),
        P(),
        P(),
    )
    out_specs = P(("ctx", "tp"), None)
    return jax.shard_map(
        per_device, mesh=mesh, in_specs=in_specs, out_specs=out_specs, check_vma=False
    )
```

profile of v0, /device:TPU:0, one launch (start us, length us, event | category | flops | bytes accessed | tf_op | source)
XLA Modules:
  0.0 467.0 jit_solution(9747930731905477069)
XLA Ops:
  6.5 0.7 all-gather.10.cloned.1.call-update
  7.3 1.7 fusion.18
  9.0 2.8 fusion.20
  11.9 0.7 all-gather.8.cloned.1.call-update
  12.6 0.5 all-gather.12.cloned.1.call-update
  13.2 0.5 all-gather.14.cloned.1.call-update
  13.9 1.0 multiply_cosine_fusion
  15.3 1.2 fusion.13
  16.5 2.0 fusion.15
  18.5 28.1 %all-gather.10.cloned.1.call-done = bf16[5376,256]{1,0:T(8,128)(2,1)} async-done(((bf16[336,256]{1,0:T(8,128)(2,1)}), bf16[5376,256]{1,0:T(8,128)(2,1)}) %all-gather.10.cloned.1.call-update) | async-done | bytes 2752528 | tf_op jit(solution)/shard_map/all_gather | solution.py:104
  46.5 132.4 %all-gather.6.cloned.1.call-done = bf16[1024,5376]{1,0:T(8,128)(2,1)} async-done(((bf16[128,5376]{1,0:T(8,128)(2,1)}), bf16[1024,5376]{1,0:T(8,128)(2,1)}) %all-gather.6.cloned.1.call-update) | async-done | bytes 11010064 | tf_op jit(solution)/shard_map/all_gather | solution.py:96
  178.9 9.0 %multiply_reduce_fusion.1 = (f32[1024,2]{0,1:T(2,128)S(1)}, f32[1024,256]{0,1:T(8,128)}) fusion(bf16[1024,5376]{1,0:T(8,128)(2,1)} %all-gather.6.cloned.1.call-done, bf16[5376,256]{1,0:T(8,128)(2,1)} %all-gather.10.cloned.1.call-done), kind=kOutput, calls=%fused_computation.58 | convolution fusion | flops 2819094528 | bytes 14819328 | tf_op jit(solution)/shard_map/dot_general | solution.py:71
  187.9 1.5 copy.17
  189.8 0.5 subtract_convert_fusion.1
  190.3 1.1 pad_maximum_fusion.2
  191.4 1.3 collective-permute-start.1
  192.7 24.8 %all-gather.8.cloned.1.call-done = bf16[5376,256]{1,0:T(8,128)(2,1)} async-done(((bf16[336,256]{1,0:T(8,128)(2,1)}), bf16[5376,256]{1,0:T(8,128)(2,1)}) %all-gather.8.cloned.1.call-update) | async-done | bytes 2752528 | tf_op jit(solution)/shard_map/all_gather | solution.py:105
  217.6 8.8 %convolution_convert_fusion.1 = bf16[1024,256]{0,1:T(8,128)(2,1)} fusion(bf16[1024,5376]{1,0:T(8,128)(2,1)} %all-gather.6.cloned.1.call-done, bf16[5376,256]{1,0:T(8,128)(2,1)} %all-gather.8.cloned.1.call-done), kind=kOutput, calls=%fused_computation.44 | convolution fusion | flops 2818834432 | bytes 14286848 | tf_op jit(solution)/shard_map/dot_general | solution.py:71
  226.3 3.1 collective-permute-start
  229.4 35.3 %all-gather.12.cloned.1.call-done = bf16[5376,512]{1,0:T(8,128)(2,1)} async-done(((bf16[336,512]{1,0:T(8,128)(2,1)}), bf16[5376,512]{1,0:T(8,128)(2,1)}) %all-gather.12.cloned.1.call-update) | async-done | bytes 5505040 | tf_op jit(solution)/shard_map/all_gather | solution.py:103
  264.7 10.3 %multiply_reduce_fusion = (f32[1024,4]{0,1:T(4,128)S(1)}, f32[1024,512]{0,1:T(8,128)S(1)}) fusion(bf16[1024,5376]{1,0:T(8,128)(2,1)} %all-gather.6.cloned.1.call-done, bf16[5376,512]{1,0:T(8,128)(2,1)} %all-gather.12.cloned.1.call-done), kind=kOutput, calls=%fused_computation.39 | convolution fusion | flops 5638189056 | bytes 18628608 | tf_op jit(solution)/shard_map/dot_general | solution.py:71
  275.1 0.5 multiply_multiply_fusion
  275.9 1.1 fusion.39
  277.3 9.5 %fusion.51 = (f32[2,2,512]{2,1,0:T(2,128)S(1)}, f32[2,2,512,1536]{2,3,1,0:T(8,128)}) fusion(pred[512,1536]{0,1:T(8,128)(4,1)S(1)} %fusion.13, bf16[512,2,2,128]{0,3,2,1:T(8,128)(2,1)} %bitcast.89, bf16[2048,2,128]{2,0,1:T(8,128)(2,1)S(1)} %maximum_maximum_fusion), kind=kOutput, calls=%fused_computation.93 | convolution fusion | flops 821036544 | bytes 15474688 | tf_op jit(solution)/shard_map/sub | solution.py:47
  286.8 8.3 %fusion.50 = (f32[2,2,512]{2,1,0:T(2,128)S(1)}, f32[2,2,512,1536]{2,3,1,0:T(8,128)}) fusion(pred[512,1536]{0,1:T(8,128)(4,1)S(1)} %copy-done.1, bf16[512,2,2,128]{0,3,2,1:T(8,128)(2,1)S(1)} %bitcast.88, bf16[2048,2,128]{2,0,1:T(8,128)(2,1)S(1)} %maximum_maximum_fusion), kind=kOutput, calls=%fused_computation.92 | convolution fusion | flops 821036544 | bytes 15474688 | tf_op jit(solution)/shard_map/sub | solution.py:47
  295.1 6.2 %fusion.26 = bf16[2,128,2,512]{3,1,2,0:T(8,128)(2,1)S(1)} fusion(f32[2,2,512,1536]{2,3,1,0:T(8,128)} %get-tuple-element.24, f32[2,2,512]{2,1,0:T(2,128)S(1)} %get-tuple-element.23, bf16[1024,2,128]{0,2,1:T(8,128)(2,1)} %bitcast, bf16[1024,2,128]{0,2,1:T(8,128)(2,1)} %collective-permute-done), kind=kOutput, calls=%fused_computation.42 | convolution fusion | flops 813432832 | bytes 14163968 | tf_op jit(solution)/shard_map/hgrk,khd->rhgd/dot_general | solution.py:49
  301.4 2.6 copy-done.6
  304.0 2.2 fusion.27
  306.3 11.5 %convolution_convert_fusion = bf16[1024,5376]{1,0:T(8,128)(2,1)} fusion(bf16[512,5376]{0,1:T(8,128)(2,1)} %all-gather.14.cloned.1.call-done, bf16[512,512]{0,1:T(8,128)(2,1)S(1)} %bitcast.90, bf16[512,512]{0,1:T(8,128)(2,1)S(1)} %bitcast.91), kind=kOutput, calls=%fused_computation.8 | convolution fusion | flops 5644746752 | bytes 17563648 | tf_op jit(solution)/shard_map/dot_general | solution.py:117
  317.9 137.5 %reduce-scatter.2.cloned.1.call-done = bf16[128,5376]{1,0:T(8,128)(2,1)} async-done(((bf16[1024,5376]{1,0:T(8,128)(2,1)}), bf16[128,5376]{1,0:T(8,128)(2,1)}) %reduce-scatter.2.cloned.1.call-update) | async-done | bytes 1376272 | tf_op jit(solution)/shard_map/reduce_scatter | solution.py:116
  455.4 1.7 fusion.16
  457.1 3.0 fusion.21
  (39 shorter events, 1.9 us)
Async XLA Ops:
  6.5 40.0 %all-gather.10.cloned.1.call-start = ((), (), s32[]{:S(2)}) async-start(), calls=%async_computation.3 | async-start | bytes 2924544 | tf_op jit(solution)/shard_map/all_gather | solution.py:104
  7.3 171.6 %all-gather.6.cloned.1.call-start = ((), (), s32[]{:S(2)}) async-start(), calls=%async_computation.1 | async-start | bytes 12386304 | tf_op jit(solution)/shard_map/all_gather | solution.py:96
  11.8 205.7 %all-gather.8.cloned.1.call-start = ((), (), s32[]{:S(2)}) async-start(), calls=%async_computation.2 | async-start | bytes 2924544 | tf_op jit(solution)/shard_map/all_gather | solution.py:105
  12.6 252.1 %all-gather.12.cloned.1.call-start = ((), (), s32[]{:S(2)}) async-start(), calls=%async_computation.4 | async-start | bytes 5849088 | tf_op jit(solution)/shard_map/all_gather | solution.py:103
  13.1 293.2 %all-gather.14.cloned.1.call-start = ((), (), s32[]{:S(2)}) async-start(), calls=%async_computation.5 | async-start | bytes 5849088 | tf_op jit(solution)/shard_map/all_gather | solution.py:115
  13.7 441.7 %reduce-scatter.2.cloned.1.call-start = ((), (), s32[]{:S(2)}) async-start(), calls=%async_computation.6 | async-start | bytes 12386304 | tf_op jit(solution)/shard_map/reduce_scatter | solution.py:116
  18.5 171.0 %copy-start.4 = (f32[128]{0:T(128)S(1)}, f32[128]{0:T(128)}, u32[]{:S(2)}) copy-start(f32[128]{0:T(128)} %param.16) | copy-start | bytes 1540
  191.4 85.6 %collective-permute-start.1 = (bf16[1024,2,128]{2,0,1:T(8,128)(2,1)}, bf16[1024,2,128]{2,0,1:T(8,128)(2,1)S(1)}, u32[]{:S(2)}, u32[]{:S(2)}) collective-permute-start(bf16[1024,2,128]{2,0,1:T(8,128)(2,1)} %pad_maximum_fusion.2), channel_id=1, source_target_pairs={{0,8},{8,16},{16,24},{24,32},{32,40},{40,48},{48,56},{56,64},{64,7... | collective-permute-start | bytes 1572872 | tf_op jit(solution)/shard_map/ppermute | solution.py:13
  226.3 48.7 %copy-start.5 = (f32[128]{0:T(128)S(1)}, f32[128]{0:T(128)}, u32[]{:S(2)}) copy-start(f32[128]{0:T(128)} %param.15) | copy-start | bytes 1540
  226.3 68.8 %collective-permute-start = (bf16[1024,2,128]{0,2,1:T(8,128)(2,1)}, bf16[1024,2,128]{0,2,1:T(8,128)(2,1)}, u32[]{:S(2)}, u32[]{:S(2)}) collective-permute-start(bf16[1024,2,128]{0,2,1:T(8,128)(2,1)} %bitcast), channel_id=1, source_target_pairs={{0,8},{8,16},{16,24},{24,32},{32,40},{40,48},{48,56},{56,64},{64,7... | collective-permute-start | bytes 1572872 | tf_op jit(solution)/shard_map/ppermute | solution.py:13
  277.3 9.5 %copy-start.1 = (pred[512,1536]{0,1:T(8,128)(4,1)S(1)}, pred[512,1536]{0,1:T(8,128)(4,1)}, u32[]{:S(2)}) copy-start(pred[512,1536]{0,1:T(8,128)(4,1)} %fusion.15) | copy-start | bytes 2359300
  277.3 9.5 %copy-start.2 = (bf16[512,4,128]{0,2,1:T(8,128)(2,1)S(1)}, bf16[512,4,128]{0,2,1:T(8,128)(2,1)}, u32[]{:S(2)}) copy-start(bf16[512,4,128]{0,2,1:T(8,128)(2,1)} %get-tuple-element.10) | copy-start | bytes 1572868
  295.1 8.9 %copy-start.6 = (f32[2,2,512,1536]{2,3,1,0:T(8,128)S(1)}, f32[2,2,512,1536]{2,3,1,0:T(8,128)}, u32[]{:S(2)}) copy-start(f32[2,2,512,1536]{2,3,1,0:T(8,128)} %get-tuple-element.26) | copy-start | bytes 37748740
  317.9 139.2 %copy-start = (bf16[128,5376]{1,0:T(8,128)(2,1)S(1)}, bf16[128,5376]{1,0:T(8,128)(2,1)}, u32[]{:S(2)}) copy-start(bf16[128,5376]{1,0:T(8,128)(2,1)} %param.9) | copy-start | bytes 4128772
  317.9 139.2 %copy-start.3 = (f32[5376]{0:T(1024)S(1)}, f32[5376]{0:T(1024)}, u32[]{:S(2)}) copy-start(f32[5376]{0:T(1024)} %param.17) | copy-start | bytes 64516
Sparse Core Ops, SparseCore 0:
  9.0 37.4 all-gather.9
  48.8 130.0 all-gather.5
  180.6 36.9 all-gather.7
  219.1 45.5 all-gather.11
  266.2 40.0 all-gather.13
  318.0 137.3 reduce-scatter.1
where the time goes:
time: 467 us
  waiting for transfers between devices  361 us (77%)
  matrix products  65.9 us (14%)
  other arithmetic  17.5 us (4%)
  between operations  13.7 us (3%)
    reduce_scatter x1, waiting for transfers between devices, per_device(): lax.psum_scatter(jnp.dot(attended, out_full, preferred_element_type=jnp.f...  138 us
    all_gather x1, waiting for transfers between devices, per_device(): block = lax.all_gather(normed, 'tp', axis=0, tiled=True)  132 us
    all_gather x1, waiting for transfers between devices, per_device(): lax.all_gather(query_weight, 'ctx', axis=0, tiled=True)  35.3 us
    dot_general x3, matrix products, add_product(): return jnp.dot(left, weight_piece, preferred_element_type=jnp.float32)  28.1 us
    all_gather x1, waiting for transfers between devices, per_device(): lax.all_gather(key_weight, 'ctx', axis=0, tiled=True)  28.1 us
    all_gather x1, waiting for transfers between devices, per_device(): lax.all_gather(value_weight, 'ctx', axis=0, tiled=True)  24.8 us
    sub x2, matrix products, attend(): expo = jnp.where(allowed, jnp.exp(scores - row_max), 0.0)  17.8 us
    dot_general x1, matrix products, per_device(): jnp.dot(attended, out_full, preferred_element_type=jnp.float32)  11.5 us
  transfers between devices with their start and end apart: 8, of which 6 were waited for; matrix products, arithmetic and copies ran while one was open for 15% of the time, Pallas kernels for 0%

commit v1 on v0

--- a/solution.py
+++ b/solution.py
@@ -101,7 +101,12 @@
     wide_pos = block_start - WINDOW + jnp.arange(WINDOW + block_rows, dtype=jnp.int32)
     kv_rows = block.shape[0]
     query_raw = add_product(block, lax.all_gather(query_weight, "ctx", axis=0, tiled=True))
-    key_raw = add_product(block, lax.all_gather(key_weight, "ctx", axis=0, tiled=True))
+    key_raw = add_product(
+        block,
+        jnp.concatenate(
+            lax.all_to_all(jnp.stack([key_weight] * lax.axis_size("ctx")), "ctx", 0, 0), axis=0
+        ),
+    )
     value_raw = add_product(block, lax.all_gather(value_weight, "ctx", axis=0, tiled=True))
     queries = rotate(
         rms_scale(query_raw.reshape(block_rows, -1, head_dim), q_gain), own_pos

time: 467 us -> 449 us (0.961)
  waiting for transfers between devices: 361 us -> 332 us
  starting transfers between devices: 4.57 us -> 11.8 us
    all_gather x1, waiting for transfers between devices: 132 us -> 85.7 us  [per_device(): block = lax.all_gather(normed, 'tp', axis=0, tiled=True)]
    all_to_all x0 -> x1, waiting for transfers between devices: none -> 43.9 us  [per_device(): lax.all_to_all(jnp.stack([key_weight] * lax.axis_size('ctx')), 'ctx', 0, 0)]
    all_gather x1 -> x0, waiting for transfers between devices: 28.1 us -> none  [per_device(): lax.all_gather(key_weight, 'ctx', axis=0, tiled=True)]
    all_to_all x0 -> x1, starting transfers between devices: none -> 6.46 us  [per_device(): lax.all_to_all(jnp.stack([key_weight] * lax.axis_size('ctx')), 'ctx', 0, 0)]
    all_gather x1, waiting for transfers between devices: 24.8 us -> 30 us  [per_device(): lax.all_gather(value_weight, 'ctx', axis=0, tiled=True)]
  transfers between devices with their start and end apart: 8 -> 8, of which waited for: 6 -> 5; matrix products, arithmetic and copies ran while one was open for 15% -> 15% of each run, Pallas kernels for 0% -> 0%
where the time goes in v1:
time: 449 us; the launch traced here: 448 us
  waiting for transfers between devices  332 us (74%)
  matrix products  65.1 us (14%)
  other arithmetic  18.4 us (4%)
  between operations  13.4 us (3%)
  starting transfers between devices  11.8 us (3%)
  local copies, waits for them, and re-layouts  7.27 us (2%)
    reduce_scatter x1, waiting for transfers between devices, per_device(): lax.psum_scatter(jnp.dot(attended, out_full, preferred_element_type=jnp.f...  137 us
    all_gather x1, waiting for transfers between devices, per_device(): block = lax.all_gather(normed, 'tp', axis=0, tiled=True)  85.7 us
    all_to_all x1, waiting for transfers between devices, per_device(): lax.all_to_all(jnp.stack([key_weight] * lax.axis_size('ctx')), 'ctx', 0, 0)  43.9 us
    all_gather x1, waiting for transfers between devices, per_device(): lax.all_gather(query_weight, 'ctx', axis=0, tiled=True)  33.3 us
    all_gather x1, waiting for transfers between devices, per_device(): lax.all_gather(value_weight, 'ctx', axis=0, tiled=True)  30 us
    dot_general x3, matrix products, add_product(): return jnp.dot(left, weight_piece, preferred_element_type=jnp.float32)  25.8 us
    sub x2, matrix products, attend(): expo = jnp.where(allowed, jnp.exp(scores - row_max), 0.0)  19.3 us
    dot_general x1, matrix products, per_device(): jnp.dot(attended, out_full, preferred_element_type=jnp.float32)  11.6 us
  transfers between devices with their start and end apart: 8, of which 5 were waited for; matrix products, arithmetic and copies ran while one was open for 15% of the time, Pallas kernels for 0%

profile of v1, /device:TPU:0, one launch (start us, length us, event | category | flops | bytes accessed | tf_op | source)
XLA Modules:
  0.0 448.1 jit_solution(12771011128860663403)
XLA Ops:
  6.5 1.7 fusion.20
  8.3 2.8 fusion.22
  11.2 0.7 all-gather.7.cloned.1.call-update
  11.9 0.7 all-gather.9.cloned.1.call-update
  12.6 1.7 stack.2
  14.3 6.5 %all-to-all-start = ((bf16[16,336,256]{2,1,0:T(8,128)(2,1)}), bf16[16,336,256]{2,1,0:T(8,128)(2,1)S(1)}, u32[]{:S(2)}, u32[]{:S(2)}) async-start(bf16[16,336,256]{2,1,0:T(8,128)(2,1)} %stack.2), calls=%async_computation | async-start | bytes 5505024 | tf_op jit(solution)/shard_map/all_to_all | solution.py:107
  20.9 0.5 all-gather.11.cloned.1.call-update
  21.5 1.0 multiply_cosine_fusion
  22.5 2.0 fusion.15
  24.5 1.9 fusion.17
  26.4 43.9 %all-to-all-done = bf16[16,336,256]{2,1,0:T(8,128)(2,1)S(1)} async-done(((bf16[16,336,256]{2,1,0:T(8,128)(2,1)}), bf16[16,336,256]{2,1,0:T(8,128)(2,1)S(1)}, u32[]{:S(2)}, u32[]{:S(2)}) %all-to-all-start) | async-done | bytes 2752544 | tf_op jit(solution)/shard_map/all_to_all | solution.py:107
  70.3 2.9 copy.17
  73.3 85.7 %all-gather.5.cloned.1.call-done = bf16[1024,5376]{1,0:T(8,128)(2,1)} async-done(((bf16[128,5376]{1,0:T(8,128)(2,1)}), bf16[1024,5376]{1,0:T(8,128)(2,1)}) %all-gather.5.cloned.1.call-update) | async-done | bytes 11010064 | tf_op jit(solution)/shard_map/all_gather | solution.py:96
  159.0 6.7 %multiply_reduce_fusion.1 = (f32[1024,2]{0,1:T(2,128)S(1)}, f32[1024,2,128]{0,2,1:T(8,128)S(1)}) fusion(bf16[2,128,5376]{2,1,0:T(8,128)(2,1)} %bitcast.94, bf16[1024,5376]{1,0:T(8,128)(2,1)} %all-gather.5.cloned.1.call-done), kind=kOutput, calls=%fused_computation.58 | convolution fusion | flops 2819094528 | bytes 14819328 | tf_op jit(solution)/shard_map/dot_general | solution.py:71
  166.1 0.8 pad_maximum_fusion.2
  166.9 2.1 collective-permute-start.1
  169.0 30.0 %all-gather.7.cloned.1.call-done = bf16[5376,256]{1,0:T(8,128)(2,1)} async-done(((bf16[336,256]{1,0:T(8,128)(2,1)}), bf16[5376,256]{1,0:T(8,128)(2,1)}) %all-gather.7.cloned.1.call-update) | async-done | bytes 2752528 | tf_op jit(solution)/shard_map/all_gather | solution.py:110
  199.1 8.7 %convolution_convert_fusion.1 = bf16[1024,256]{0,1:T(8,128)(2,1)} fusion(bf16[1024,5376]{1,0:T(8,128)(2,1)} %all-gather.5.cloned.1.call-done, bf16[5376,256]{1,0:T(8,128)(2,1)} %all-gather.7.cloned.1.call-done), kind=kOutput, calls=%fused_computation.46 | convolution fusion | flops 2818834432 | bytes 14286848 | tf_op jit(solution)/shard_map/dot_general | solution.py:71
  207.8 3.1 collective-permute-start
  210.9 33.3 %all-gather.9.cloned.1.call-done = bf16[5376,512]{1,0:T(8,128)(2,1)} async-done(((bf16[336,512]{1,0:T(8,128)(2,1)}), bf16[5376,512]{1,0:T(8,128)(2,1)}) %all-gather.9.cloned.1.call-update) | async-done | bytes 5505040 | tf_op jit(solution)/shard_map/all_gather | solution.py:103
  244.2 10.3 %multiply_reduce_fusion = (f32[1024,4]{0,1:T(4,128)S(1)}, f32[1024,512]{0,1:T(8,128)S(1)}) fusion(bf16[1024,5376]{1,0:T(8,128)(2,1)} %all-gather.5.cloned.1.call-done, bf16[5376,512]{1,0:T(8,128)(2,1)} %all-gather.9.cloned.1.call-done), kind=kOutput, calls=%fused_computation.41 | convolution fusion | flops 5638189056 | bytes 18628608 | tf_op jit(solution)/shard_map/dot_general | solution.py:71
  255.5 1.1 fusion.41
  256.6 1.1 maximum_maximum_fusion
  257.7 10.2 %fusion.53 = (f32[2,2,512]{2,1,0:T(2,128)S(1)}, f32[2,2,512,1536]{2,3,1,0:T(8,128)}) fusion(pred[512,1536]{0,1:T(8,128)(4,1)S(1)} %copy-done.1, bf16[512,2,2,128]{0,3,2,1:T(8,128)(2,1)} %bitcast.96, bf16[2048,2,128]{0,2,1:T(8,128)(2,1)S(1)} %maximum_maximum_fusion), kind=kOutput, calls=%fused_computation.95 | convolution fusion | flops 821036544 | bytes 15474688 | tf_op jit(solution)/shard_map/sub | solution.py:47
  267.9 9.1 %fusion.52 = (f32[2,2,512]{2,1,0:T(2,128)S(1)}, f32[2,2,512,1536]{2,3,1,0:T(8,128)}) fusion(pred[512,1536]{0,1:T(8,128)(4,1)S(1)} %copy-done.2, bf16[512,2,2,128]{0,3,2,1:T(8,128)(2,1)S(1)} %bitcast.95, bf16[2048,2,128]{0,2,1:T(8,128)(2,1)S(1)} %maximum_maximum_fusion), kind=kOutput, calls=%fused_computation.94 | convolution fusion | flops 821036544 | bytes 15474688 | tf_op jit(solution)/shard_map/sub | solution.py:47
  277.0 6.2 %fusion.28 = bf16[2,128,2,512]{3,1,2,0:T(8,128)(2,1)S(1)} fusion(f32[2,2,512,1536]{2,3,1,0:T(8,128)} %get-tuple-element.24, f32[2,2,512]{2,1,0:T(2,128)S(1)} %get-tuple-element.23, bf16[1024,2,128]{0,2,1:T(8,128)(2,1)} %bitcast, bf16[1024,2,128]{0,2,1:T(8,128)(2,1)} %collective-permute-done), kind=kOutput, calls=%fused_computation.44 | convolution fusion | flops 813432832 | bytes 14163968 | tf_op jit(solution)/shard_map/hgrk,khd->rhgd/dot_general | solution.py:49
  283.3 2.6 copy-done.8
  285.8 2.2 fusion.29
  288.0 11.6 %convolution_convert_fusion = bf16[1024,5376]{1,0:T(8,128)(2,1)} fusion(bf16[512,5376]{0,1:T(8,128)(2,1)} %all-gather.11.cloned.1.call-done, bf16[512,512]{0,1:T(8,128)(2,1)S(1)} %bitcast.97, bf16[512,512]{0,1:T(8,128)(2,1)S(1)} %bitcast.98), kind=kOutput, calls=%fused_computation.8 | convolution fusion | flops 5644746752 | bytes 17563648 | tf_op jit(solution)/shard_map/dot_general | solution.py:122
  299.7 137.2 %reduce-scatter.2.cloned.1.call-done = bf16[128,5376]{1,0:T(8,128)(2,1)} async-done(((bf16[1024,5376]{1,0:T(8,128)(2,1)}), bf16[128,5376]{1,0:T(8,128)(2,1)}) %reduce-scatter.2.cloned.1.call-update) | async-done | bytes 1376272 | tf_op jit(solution)/shard_map/reduce_scatter | solution.py:121
  436.9 1.7 fusion.18
  438.6 3.0 fusion.23
  (41 shorter events, 1.5 us)
Async XLA Ops:
  6.5 6.1 %copy-start.4 = (bf16[336,256]{1,0:T(8,128)(2,1)S(1)}, bf16[336,256]{1,0:T(8,128)(2,1)}, u32[]{:S(2)}) copy-start(bf16[336,256]{1,0:T(8,128)(2,1)} %param.12) | copy-start | bytes 516100
  6.5 152.5 %all-gather.5.cloned.1.call-start = ((), (), s32[]{:S(2)}) async-start(), calls=%async_computation.2 | async-start | bytes 12386304 | tf_op jit(solution)/shard_map/all_gather | solution.py:96
  11.1 187.9 %all-gather.7.cloned.1.call-start = ((), (), s32[]{:S(2)}) async-start(), calls=%async_computation.3 | async-start | bytes 2924544 | tf_op jit(solution)/shard_map/all_gather | solution.py:110
  11.9 232.4 %all-gather.9.cloned.1.call-start = ((), (), s32[]{:S(2)}) async-start(), calls=%async_computation.4 | async-start | bytes 5849088 | tf_op jit(solution)/shard_map/all_gather | solution.py:103
  14.3 56.0 %all-to-all-start = ((bf16[16,336,256]{2,1,0:T(8,128)(2,1)}), bf16[16,336,256]{2,1,0:T(8,128)(2,1)S(1)}, u32[]{:S(2)}, u32[]{:S(2)}) async-start(bf16[16,336,256]{2,1,0:T(8,128)(2,1)} %stack.2), calls=%async_computation | async-start | bytes 5505024 | tf_op jit(solution)/shard_map/all_to_all | solution.py:107
  20.8 267.2 %all-gather.11.cloned.1.call-start = ((), (), s32[]{:S(2)}) async-start(), calls=%async_computation.5 | async-start | bytes 5849088 | tf_op jit(solution)/shard_map/all_gather | solution.py:120
  21.4 415.5 %reduce-scatter.2.cloned.1.call-start = ((), (), s32[]{:S(2)}) async-start(), calls=%async_computation.6 | async-start | bytes 12386304 | tf_op jit(solution)/shard_map/reduce_scatter | solution.py:121
  159.0 6.7 %copy-start.6 = (f32[128]{0:T(128)S(1)}, f32[128]{0:T(128)}, u32[]{:S(2)}) copy-start(f32[128]{0:T(128)} %param.16) | copy-start | bytes 1540
  166.9 89.6 %collective-permute-start.1 = (bf16[1024,2,128]{0,2,1:T(8,128)(2,1)}, bf16[1024,2,128]{0,2,1:T(8,128)(2,1)}, u32[]{:S(2)}, u32[]{:S(2)}) collective-permute-start(bf16[1024,2,128]{0,2,1:T(8,128)(2,1)} %pad_maximum_fusion.2), channel_id=1, source_target_pairs={{0,8},{8,16},{16,24},{24,32},{32,40},{40,48},{48,56},{56,64},{64,7... | collective-permute-start | bytes 1572872 | tf_op jit(solution)/shard_map/ppermute | solution.py:13
  207.8 46.8 %copy-start.7 = (f32[128]{0:T(128)S(1)}, f32[128]{0:T(128)}, u32[]{:S(2)}) copy-start(f32[128]{0:T(128)} %param.15) | copy-start | bytes 1540
  207.8 69.2 %collective-permute-start = (bf16[1024,2,128]{0,2,1:T(8,128)(2,1)}, bf16[1024,2,128]{0,2,1:T(8,128)(2,1)}, u32[]{:S(2)}, u32[]{:S(2)}) collective-permute-start(bf16[1024,2,128]{0,2,1:T(8,128)(2,1)} %bitcast), channel_id=1, source_target_pairs={{0,8},{8,16},{16,24},{24,32},{32,40},{40,48},{48,56},{56,64},{64,7... | collective-permute-start | bytes 1572872 | tf_op jit(solution)/shard_map/ppermute | solution.py:13
  255.1 2.6 copy-start.1
  257.7 10.2 %copy-start.2 = (pred[512,1536]{0,1:T(8,128)(4,1)S(1)}, pred[512,1536]{0,1:T(8,128)(4,1)}, u32[]{:S(2)}) copy-start(pred[512,1536]{0,1:T(8,128)(4,1)} %fusion.17) | copy-start | bytes 2359300
  257.7 10.2 %copy-start.3 = (bf16[512,4,128]{0,2,1:T(8,128)(2,1)S(1)}, bf16[512,4,128]{0,2,1:T(8,128)(2,1)}, u32[]{:S(2)}) copy-start(bf16[512,4,128]{0,2,1:T(8,128)(2,1)} %get-tuple-element.10) | copy-start | bytes 1572868
  277.0 8.8 %copy-start.8 = (f32[2,2,512,1536]{2,3,1,0:T(8,128)S(1)}, f32[2,2,512,1536]{2,3,1,0:T(8,128)}, u32[]{:S(2)}) copy-start(f32[2,2,512,1536]{2,3,1,0:T(8,128)} %get-tuple-element.26) | copy-start | bytes 37748740
  299.6 139.0 %copy-start = (bf16[128,5376]{1,0:T(8,128)(2,1)S(1)}, bf16[128,5376]{1,0:T(8,128)(2,1)}, u32[]{:S(2)}) copy-start(bf16[128,5376]{1,0:T(8,128)(2,1)} %param.9) | copy-start | bytes 4128772
  299.6 139.0 %copy-start.5 = (f32[5376]{0:T(1024)S(1)}, f32[5376]{0:T(1024)}, u32[]{:S(2)}) copy-start(f32[5376]{0:T(1024)} %param.17) | copy-start | bytes 64516
Sparse Core Ops, SparseCore 0:
  11.2 147.7 all-gather.4
  160.7 38.3 all-gather.6
  200.8 43.4 all-gather.8
  245.8 39.9 all-gather.10
  299.8 137.0 reduce-scatter.1
